TPU v7x, 32 devices: a whole 2x2x4 slice. The times are simulated.
32 devices in a mesh: tok: 2 (over core), head: 4 (over y, x), exp: 4 (over z).
Axes of the slice: x: 2, y: 2, z: 4, core: 2. Of those that a mesh axis runs over, the one named last changes fastest.
Arguments:
- context: bfloat16 [4, 64, 4096], P('exp', 'tok', 'head'), may hold values from -6 to 6
- out_proj: bfloat16 [4096, 4096], P('head', 'exp'), may hold values from -0.125 to 0.125
- stream: float32 [4, 64, 4096], P('exp', 'tok', 'head'), may hold values from -75 to 75
- norm_gain: float32 [4096], replicated, may hold values from 0.1 to 1.9
- expert_ids: int32 [4, 64, 8], P('exp', 'tok'), may hold values from 0 to 31, as said below
- slot_ids: int32 [4, 64, 8], P('exp', 'tok'), may hold values from -1 to 11, as said below
- gate_probs: float32 [4, 64, 8], P('exp', 'tok'), may hold values from 0.02 to 0.3
- w_gate: bfloat16 [32, 3072, 4096], P(('tok', 'exp'), 'head'), may hold values from -0.09375 to 0.09375
- w_up: bfloat16 [32, 3072, 4096], P(('tok', 'exp'), 'head'), may hold values from -0.09375 to 0.09375
- w_down: bfloat16 [32, 3072, 4096], P(('tok', 'exp'), 'head'), may hold values from -0.15625 to 0.15625
Outputs:
- mixed: float32 [4, 64, 4096], P('exp', 'tok', 'head')
Inputs may be any that keep to these rules, and one draw needn't show every extreme that they name: `expert_ids`: each token names 8 different experts. `slot_ids`: within a block of 32 consecutive tokens of one image, the choices of one expert take slots 0, 1, 2, ... in token order until its 12 slots are full, later ones get -1; in every block some expert fills all 12 slots.
All inputs are finite; a program needn't handle non-finite values.
Results may differ from a plain program's by a relative error of at most 0.0034.
Values may be sent and summed in bfloat16 or wider, within the bound.
A program may use at most 128 MiB of HBM per device.

v0:
```python
import jax
import jax.numpy as jnp
from jax import lax
from jax.sharding import PartitionSpec as P

EXPERTS = 32
TOP = 8
CAP = 12
eps_value = 1e-05


def on_device(
    context, out_proj, stream, norm_gain, expert_ids, slot_ids, gate_probs, w_gate, w_up, w_down
):
    local_context = context[0]
    own_stream = stream[0]
    col_width = own_stream.shape[1]
    col_start = lax.axis_index("head") * col_width
    partial_value = jnp.dot(
        local_context,
        lax.all_gather(out_proj, "exp", axis=1, tiled=True),
        preferred_element_type=jnp.float32,
    )
    own_sum = lax.dynamic_slice_in_dim(partial_value, col_start, col_width, 1) + own_stream
    partial_value = lax.dynamic_update_slice_in_dim(partial_value, own_sum, col_start, 1)
    resid_full = lax.psum(partial_value, "head")
    resid_own = lax.dynamic_slice_in_dim(resid_full, col_start, col_width, 1)
    mean_sq = jnp.mean(resid_full * resid_full, axis=1, keepdims=True)
    gain_own = lax.dynamic_slice_in_dim(norm_gain, col_start, col_width, 0)
    normed_own = (resid_own * lax.rsqrt(mean_sq + eps_value) * gain_own).astype(jnp.bfloat16)
    choice_ids = expert_ids[0]
    choice_slots = slot_ids[0]
    weights = gate_probs[0]
    spill_slot = EXPERTS * CAP
    target = jnp.where(choice_slots >= 0, choice_ids * CAP + choice_slots, spill_slot)
    outgoing = (
        jnp.zeros((spill_slot + 1, col_width), jnp.bfloat16)
        .at[target.reshape(-1)]
        .set(jnp.repeat(normed_own, TOP, axis=0))
    )
    outgoing = outgoing[:spill_slot].reshape(EXPERTS, CAP, col_width)
    tok_count = lax.axis_size("tok")
    groups = tok_count * lax.axis_size("exp")
    local_experts = w_gate.shape[0]
    arrived = lax.all_to_all(outgoing, ("tok", "exp"), split_axis=0, concat_axis=0, tiled=True)
    arrived = arrived.reshape(groups, local_experts, CAP, col_width)
    piece = lax.all_gather(arrived, "head", axis=3, tiled=True)
    gate_more = jnp.einsum("slcd,lhd->slch", piece, w_gate, preferred_element_type=jnp.float32)
    up_more = jnp.einsum("slcd,lhd->slch", piece, w_up, preferred_element_type=jnp.float32)
    hidden = (jax.nn.silu(gate_more) * up_more).astype(jnp.bfloat16)
    produced = jnp.einsum(
        "slch,lhd->slcd", hidden, w_down, preferred_element_type=jnp.float32
    ).astype(jnp.bfloat16)
    widened = lax.optimization_barrier(produced).astype(jnp.float32)
    summed = lax.psum_scatter(
        widened.astype(jnp.bfloat16), "head", scatter_dimension=3, tiled=True
    ).astype(jnp.float32)
    returned_share = lax.all_to_all(
        summed.reshape(EXPERTS, CAP, col_width).astype(jnp.bfloat16),
        ("tok", "exp"),
        split_axis=0,
        concat_axis=0,
        tiled=True,
    ).astype(jnp.float32)
    lookup_share = jnp.concatenate(
        [returned_share.reshape(spill_slot, col_width), jnp.zeros((1, col_width), jnp.float32)],
        axis=0,
    )
    picked_share = lookup_share[target]
    expert_own = jnp.sum(picked_share * weights[:, :, None], axis=1)
    return (resid_own + expert_own)[None]


def solution(mesh):
    in_specs = (
        P("exp", "tok", "head"),
        P("head", "exp"),
        P("exp", "tok", "head"),
        P(),
        P("exp", "tok", None),
        P("exp", "tok", None),
        P("exp", "tok", None),
        P(("tok", "exp"), "head", None),
        P(("tok", "exp"), "head", None),
        P(("tok", "exp"), "head", None),
    )
    out_specs = P("exp", "tok", "head")
    return jax.shard_map(
        on_device, mesh=mesh, in_specs=in_specs, out_specs=out_specs, check_vma=False
    )
```

profile of v0, /device:TPU:0, one launch (start us, length us, event | category | flops | bytes accessed | tf_op | source)
XLA Modules:
  0.0 433.1 jit_solution(15233698592753137792)
XLA Ops:
  6.5 0.7 all-gather.3.cloned.1.call-update
  7.4 153.9 %all-gather.3.cloned.1.call-done = bf16[1024,4096]{1,0:T(8,128)(2,1)} async-done(((bf16[1024,1024]{1,0:T(8,128)(2,1)}), bf16[1024,4096]{1,0:T(8,128)(2,1)}) %all-gather.3.cloned.1.call-update) | async-done | bytes 8388624 | tf_op jit(solution)/shard_map/all_gather | solution.py:21
  161.3 4.9 %fusion.24 = f32[32,4096]{1,0:T(8,128)S(1)} fusion(bf16[1024,4096]{1,0:T(8,128)(2,1)} %all-gather.3.cloned.1.call-done, bf16[1,32,1024]{2,1,0:T(8,128)(2,1)S(1)} %copy-done), kind=kOutput, calls=%fused_computation.29 | convolution fusion | flops 268435456 | bytes 8978432 | tf_op jit(solution)/shard_map/dot_general | solution.py:19
  166.2 0.8 copy-done.2
  167.1 0.0 all-gather.5.cloned.1.call-start
  167.1 0.1 copy.19
  167.2 0.1 select_n.53
  167.3 43.5 %all-reduce.3.cloned.1.call-done = f32[32,4096]{1,0:T(8,128)} async-done(((f32[32,4096]{1,0:T(8,128)}), f32[32,4096]{1,0:T(8,128)}) %all-reduce.3.cloned.1.call-update) | async-done | bytes 524304 | tf_op jit(solution)/shard_map/psum | solution.py:26
  210.8 1.2 multiply_reduce_fusion
  212.0 1.0 multiply_convert_fusion
  213.0 1.9 scatter_custom_fusion
  214.9 0.1 slice.6
  214.9 0.2 reshape.125
  215.1 30.6 %all_to_all.10 = bf16[32,12,1024]{2,1,0:T(8,128)(2,1)S(1)} all-to-all(bf16[32,12,1024]{2,1,0:T(8,128)(2,1)S(1)} %reshape.125), channel_id=1, replica_groups=mesh['tok'=2,'head'=4,'exp'=4] {'tok','exp'}, dimensions={0} | all-to-all | bytes 1572864 | tf_op jit(solution)/shard_map/all_to_all | solution.py:45
  245.7 1.0 copy.21
  246.8 0.2 reduce-scatter.2.cloned.1.call-start
  247.0 50.0 %all-gather.5.cloned.1.call-done = bf16[8,4,12,4096]{3,2,0,1:T(8,128)(2,1)} async-done(((bf16[8,4,12,1024]{3,2,0,1:T(8,128)(2,1)}), bf16[8,4,12,4096]{3,2,0,1:T(8,128)(2,1)}) %all-gather.5.cloned.1.call-update) | async-done | bytes 3145744 | tf_op jit(solution)/shard_map/all_gather | solution.py:47
  297.0 13.4 %fusion.4 = f32[4,8,12,768]{3,2,1,0:T(8,128)S(1)} fusion(bf16[8,4,12,4096]{3,2,0,1:T(8,128)(2,1)} %all-gather.5.cloned.1.call-done, bf16[4,768,4096]{2,1,0:T(8,128)(2,1)} %param.17), kind=kOutput, calls=%fused_computation.6 | convolution fusion | flops 2415919104 | bytes 29491200 | tf_op jit(solution)/shard_map/slcd,lhd->slch/dot_general | solution.py:48
  310.4 13.5 %fusion.12 = bf16[8,4,12,768]{3,2,0,1:T(8,128)(2,1)S(1)} fusion(f32[4,8,12,768]{3,2,1,0:T(8,128)S(1)} %fusion.4, bf16[8,4,12,4096]{3,2,0,1:T(8,128)(2,1)} %all-gather.5.cloned.1.call-done, bf16[4,768,4096]{2,1,0:T(8,128)(2,1)} %param.18), kind=kOutput, calls=%fused_computation.11 | convolution fusion | flops 2417688576 | bytes 30081024 | tf_op jit(solution)/shard_map/slcd,lhd->slch/dot_general | solution.py:49
  323.9 13.6 %fusion.9 = bf16[8,4,12,4096]{3,2,0,1:T(8,128)(2,1)} fusion(bf16[8,4,12,768]{3,2,0,1:T(8,128)(2,1)S(1)} %fusion.12, bf16[4,768,4096]{2,1,0:T(8,128)(2,1)} %param.19), kind=kOutput, calls=%fused_computation.9 | convolution fusion | flops 2417491968 | bytes 28901376 | tf_op jit(solution)/shard_map/slch,lhd->slcd/dot_general | solution.py:51
  337.5 52.7 %reduce-scatter.2.cloned.1.call-done = bf16[8,4,12,1024]{3,2,0,1:T(8,128)(2,1)} async-done(((bf16[8,4,12,4096]{3,2,0,1:T(8,128)(2,1)}), bf16[8,4,12,1024]{3,2,0,1:T(8,128)(2,1)}) %reduce-scatter.2.cloned.1.call-update) | async-done | bytes 786448 | tf_op jit(solution)/shard_map/reduce_scatter | solution.py:55
  390.2 2.3 copy.31
  392.5 4.6 %all-to-all-start.1 = ((bf16[32,12,1024]{2,1,0:T(8,128)(2,1)}), bf16[32,12,1024]{2,1,0:T(8,128)(2,1)S(1)}, u32[]{:S(2)}, u32[]{:S(2)}) async-start(bf16[32,12,1024]{2,1,0:T(8,128)(2,1)} %bitcast.14), calls=%async_computation.2 | async-start | bytes 2097152 | tf_op jit(solution)/shard_map/all_to_all | solution.py:58
  397.1 0.1 copy.24
  397.2 0.1 reshape.130
  397.3 0.1 copy.25
  397.4 25.7 %all-to-all-done.1 = bf16[32,12,1024]{2,1,0:T(8,128)(2,1)S(1)} async-done(((bf16[32,12,1024]{2,1,0:T(8,128)(2,1)}), bf16[32,12,1024]{2,1,0:T(8,128)(2,1)S(1)}, u32[]{:S(2)}, u32[]{:S(2)}) %all-to-all-start.1) | async-done | bytes 786464 | tf_op jit(solution)/shard_map/all_to_all | solution.py:58
  423.1 0.2 reshape.127
  423.3 0.2 pad_convert_fusion
  423.5 1.1 gather_fusion
  424.6 0.4 fusion.18
  424.9 1.6 add_bitcast_fusion
  (25 shorter events, 0.2 us)
Async XLA Ops:
  6.5 154.7 %copy-start = (bf16[1,32,1024]{2,1,0:T(8,128)(2,1)S(1)}, bf16[1,32,1024]{2,1,0:T(8,128)(2,1)}, u32[]{:S(2)}) copy-start(bf16[1,32,1024]{2,1,0:T(8,128)(2,1)} %param.10) | copy-start | bytes 196612
  6.5 154.7 %all-gather.3.cloned.1.call-start = ((), (), s32[]{:S(2)}) async-start(), calls=%async_computation.3 | async-start | bytes 10485760 | tf_op jit(solution)/shard_map/all_gather | solution.py:21
  7.3 203.5 %all-reduce.3.cloned.1.call-start = ((), (), s32[]{:S(2)}) async-start(), calls=%async_computation.4 | async-start | bytes 1048576 | tf_op jit(solution)/shard_map/psum | solution.py:26
  7.3 158.9 %copy-start.3 = (f32[1,32,1024]{2,1,0:T(8,128)S(1)}, f32[1,32,1024]{2,1,0:T(8,128)}, u32[]{:S(2)}) copy-start(f32[1,32,1024]{2,1,0:T(8,128)} %param.12) | copy-start | bytes 393220
  7.3 159.8 %copy-start.5 = (s32[1,32,8]{1,2,0:T(8,128)S(1)}, s32[1,32,8]{1,2,0:T(8,128)}, u32[]{:S(2)}) copy-start(s32[1,32,8]{1,2,0:T(8,128)} %param.15) | copy-start | bytes 3076
  7.3 159.8 %copy-start.6 = (s32[1,32,8]{1,2,0:T(8,128)S(1)}, s32[1,32,8]{1,2,0:T(8,128)}, u32[]{:S(2)}) copy-start(s32[1,32,8]{1,2,0:T(8,128)} %param.14) | copy-start | bytes 3076
  7.3 204.6 %dynamic-slice-start = ((f32[4096]{0:T(1024)}, s32[]{:T(128)}), f32[1024]{0:T(1024)S(1)}, s32[]{:S(2)}) async-start(f32[4096]{0:T(1024)} %param.13, s32[]{:T(128)} %select_n.51), calls=%async_computation.7 | async-start | bytes 8704 | tf_op jit(solution)/shard_map/dynamic_slice | solution.py:29
  166.2 0.8 copy-start.2
  167.1 129.9 %all-gather.5.cloned.1.call-start = ((), (), s32[]{:S(2)}) async-start(), calls=%async_computation.5 | async-start | bytes 5242880 | tf_op jit(solution)/shard_map/all_gather | solution.py:47
  246.8 143.4 %reduce-scatter.2.cloned.1.call-start = ((), (), s32[]{:S(2)}) async-start(), calls=%async_computation.6 | async-start | bytes 5242880 | tf_op jit(solution)/shard_map/reduce_scatter | solution.py:55
  337.5 59.8 %copy-start.4 = (f32[1,32,8]{1,2,0:T(8,128)S(1)}, f32[1,32,8]{1,2,0:T(8,128)}, u32[]{:S(2)}) copy-start(f32[1,32,8]{1,2,0:T(8,128)} %param.16) | copy-start | bytes 3076
  392.5 30.6 %all-to-all-start.1 = ((bf16[32,12,1024]{2,1,0:T(8,128)(2,1)}), bf16[32,12,1024]{2,1,0:T(8,128)(2,1)S(1)}, u32[]{:S(2)}, u32[]{:S(2)}) async-start(bf16[32,12,1024]{2,1,0:T(8,128)(2,1)} %bitcast.14), calls=%async_computation.2 | async-start | bytes 2097152 | tf_op jit(solution)/shard_map/all_to_all | solution.py:58
  423.3 3.2 copy-start.1
Sparse Core Ops, SparseCore 0:
  8.9 152.3 all-gather.2
  167.2 43.5 all-reduce.2
  246.9 50.0 all-gather.4
  337.6 52.5 reduce-scatter.1
where the time goes:
time: 433 us
  waiting for transfers between devices  327 us (76%)
  matrix products  45.4 us (10%)
  blocking collectives  30.6 us (7%)
  between operations  13.3 us (3%)
  local copies, waits for them, and re-layouts  7.94 us (2%)
  starting transfers between devices  4.91 us (1%)
  other arithmetic  4.33 us (1%)
    all_gather x1, waiting for transfers between devices, on_device(): lax.all_gather(out_proj, 'exp', axis=1, tiled=True)  154 us
    reduce_scatter x1, waiting for transfers between devices, on_device(): lax.psum_scatter(widened.astype(jnp.bfloat16), 'head', scatter_dimension=...  52.7 us
    all_gather x1, waiting for transfers between devices, on_device(): piece = lax.all_gather(arrived, 'head', axis=3, tiled=True)  50 us
    psum x1, waiting for transfers between devices, on_device(): resid_full = lax.psum(partial_value, 'head')  43.5 us
    all_to_all x1, blocking collectives, on_device(): lax.all_to_all(outgoing, ('tok', 'exp'), split_axis=0, concat_axis=0, til...  30.6 us
    all_to_all x1, waiting for transfers between devices, on_device(): lax.all_to_all(summed.reshape(EXPERTS, CAP, col_width).astype(jnp.bfloat1...  25.7 us
    dot_general x1, matrix products, on_device(): jnp.einsum('slch,lhd->slcd', hidden, w_down, preferred_element_type=jnp.f...  13.6 us
    dot_general x1, matrix products, on_device(): jnp.einsum('slcd,lhd->slch', piece, w_up, preferred_element_type=jnp.floa...  13.5 us
  transfers between devices with their start and end apart: 5, of which 5 were waited for; matrix products, arithmetic and copies ran while one was open for 0% of the time, Pallas kernels for 0%

commit v1 on v0

--- a/solution.py
+++ b/solution.py
@@ -18,7 +18,7 @@
     col_start = lax.axis_index("head") * col_width
     partial_value = jnp.dot(
         local_context,
-        lax.all_gather(out_proj, "exp", axis=1, tiled=True),
+        jnp.concatenate(lax.all_gather(out_proj, axis_name="exp"), axis=1),
         preferred_element_type=jnp.float32,
     )
     own_sum = lax.dynamic_slice_in_dim(partial_value, col_start, col_width, 1) + own_stream

time: 433 us -> 446 us (1.030)
  local copies, waits for them, and re-layouts: 7.94 us -> 19.4 us
    reshape x0 -> x1, local copies, waits for them, and re-layouts: none -> 11.4 us  [on_device(): jnp.concatenate(lax.all_gather(out_proj, axis_name='exp'), axis=1)]
where the time goes in v1:
time: 446 us
  waiting for transfers between devices  327 us (73%)
  matrix products  46.5 us (10%)
  blocking collectives  30.6 us (7%)
  local copies, waits for them, and re-layouts  19.4 us (4%)
  between operations  13.3 us (3%)
  starting transfers between devices  4.91 us (1%)
    all_gather x1, waiting for transfers between devices, on_device(): lax.all_gather(out_proj, axis_name='exp')  154 us
    reduce_scatter x1, waiting for transfers between devices, on_device(): lax.psum_scatter(widened.astype(jnp.bfloat16), 'head', scatter_dimension=...  52.8 us
    all_gather x1, waiting for transfers between devices, on_device(): piece = lax.all_gather(arrived, 'head', axis=3, tiled=True)  50 us
    psum x1, waiting for transfers between devices, on_device(): resid_full = lax.psum(partial_value, 'head')  43.5 us
    all_to_all x1, blocking collectives, on_device(): lax.all_to_all(outgoing, ('tok', 'exp'), split_axis=0, concat_axis=0, til...  30.6 us
    all_to_all x1, waiting for transfers between devices, on_device(): lax.all_to_all(summed.reshape(EXPERTS, CAP, col_width).astype(jnp.bfloat1...  25.7 us
    dot_general x1, matrix products, on_device(): jnp.einsum('slch,lhd->slcd', hidden, w_down, preferred_element_type=jnp.f...  13.6 us
    dot_general x1, matrix products, on_device(): jnp.einsum('slcd,lhd->slch', piece, w_up, preferred_element_type=jnp.floa...  13.5 us
  transfers between devices with their start and end apart: 5, of which 5 were waited for; matrix products, arithmetic and copies ran while one was open for 0% of the time, Pallas kernels for 0%

profile of v1, /device:TPU:0, one launch (start us, length us, event | category | flops | bytes accessed | tf_op | source)
XLA Modules:
  0.0 445.6 jit_solution(1624429252074337224)
XLA Ops:
  6.5 0.7 all-gather.6.cloned.1.call-update
  7.3 154.0 %all-gather.6.cloned.1.call-done = bf16[4096,1024]{1,0:T(8,128)(2,1)} async-done(((bf16[1024,1024]{1,0:T(8,128)(2,1)}), bf16[4096,1024]{1,0:T(8,128)(2,1)}) %all-gather.6.cloned.1.call-update) | async-done | bytes 8388624 | tf_op jit(solution)/shard_map/all_gather | solution.py:21
  161.3 11.4 %copy.27 = bf16[1024,4,1024]{0,2,1:T(8,128)(2,1)} copy(bf16[1024,4,1024]{2,0,1:T(8,128)(2,1)} %bitcast.74) | data formatting | bytes 16777216 | tf_op jit(solution)/shard_map/reshape | solution.py:21
  172.7 6.0 %fusion.24 = f32[32,4096]{1,0:T(8,128)S(1)} fusion(bf16[1024,4096]{0,1:T(8,128)(2,1)} %bitcast.73, bf16[1,32,1024]{2,1,0:T(8,128)(2,1)S(1)} %copy-done), kind=kOutput, calls=%fused_computation.29 | convolution fusion | flops 268435456 | bytes 8978432 | tf_op jit(solution)/shard_map/dot_general | solution.py:19
  178.8 0.8 copy-done.2
  179.7 0.1 copy.28
  179.8 0.1 select_n.53
  179.9 43.5 %all-reduce.3.cloned.1.call-done = f32[32,4096]{1,0:T(8,128)} async-done(((f32[32,4096]{1,0:T(8,128)}), f32[32,4096]{1,0:T(8,128)}) %all-reduce.3.cloned.1.call-update) | async-done | bytes 524304 | tf_op jit(solution)/shard_map/psum | solution.py:26
  223.3 1.2 multiply_reduce_fusion
  224.5 1.0 multiply_convert_fusion
  225.5 1.9 scatter_custom_fusion
  227.4 0.1 slice.6
  227.5 0.2 reshape.133
  227.7 30.6 %all_to_all.10 = bf16[32,12,1024]{2,1,0:T(8,128)(2,1)S(1)} all-to-all(bf16[32,12,1024]{2,1,0:T(8,128)(2,1)S(1)} %reshape.133), channel_id=1, replica_groups=mesh['tok'=2,'head'=4,'exp'=4] {'tok','exp'}, dimensions={0} | all-to-all | bytes 1572864 | tf_op jit(solution)/shard_map/all_to_all | solution.py:45
  258.3 1.0 copy.30
  259.3 0.2 reduce-scatter.2.cloned.1.call-start
  259.6 50.0 %all-gather.4.cloned.1.call-done = bf16[8,4,12,4096]{3,2,0,1:T(8,128)(2,1)} async-done(((bf16[8,4,12,1024]{3,2,0,1:T(8,128)(2,1)}), bf16[8,4,12,4096]{3,2,0,1:T(8,128)(2,1)}) %all-gather.4.cloned.1.call-update) | async-done | bytes 3145744 | tf_op jit(solution)/shard_map/all_gather | solution.py:47
  309.5 13.4 %fusion.4 = f32[4,8,12,768]{3,2,1,0:T(8,128)S(1)} fusion(bf16[8,4,12,4096]{3,2,0,1:T(8,128)(2,1)} %all-gather.4.cloned.1.call-done, bf16[4,768,4096]{2,1,0:T(8,128)(2,1)} %param.17), kind=kOutput, calls=%fused_computation.6 | convolution fusion | flops 2415919104 | bytes 29491200 | tf_op jit(solution)/shard_map/slcd,lhd->slch/dot_general | solution.py:48
  323.0 13.5 %fusion.12 = bf16[8,4,12,768]{3,2,0,1:T(8,128)(2,1)S(1)} fusion(f32[4,8,12,768]{3,2,1,0:T(8,128)S(1)} %fusion.4, bf16[8,4,12,4096]{3,2,0,1:T(8,128)(2,1)} %all-gather.4.cloned.1.call-done, bf16[4,768,4096]{2,1,0:T(8,128)(2,1)} %param.18), kind=kOutput, calls=%fused_computation.11 | convolution fusion | flops 2417688576 | bytes 30081024 | tf_op jit(solution)/shard_map/slcd,lhd->slch/dot_general | solution.py:49
  336.5 13.6 %fusion.9 = bf16[8,4,12,4096]{3,2,0,1:T(8,128)(2,1)} fusion(bf16[8,4,12,768]{3,2,0,1:T(8,128)(2,1)S(1)} %fusion.12, bf16[4,768,4096]{2,1,0:T(8,128)(2,1)} %param.19), kind=kOutput, calls=%fused_computation.9 | convolution fusion | flops 2417491968 | bytes 28901376 | tf_op jit(solution)/shard_map/slch,lhd->slcd/dot_general | solution.py:51
  350.0 52.8 %reduce-scatter.2.cloned.1.call-done = bf16[8,4,12,1024]{3,2,0,1:T(8,128)(2,1)} async-done(((bf16[8,4,12,4096]{3,2,0,1:T(8,128)(2,1)}), bf16[8,4,12,1024]{3,2,0,1:T(8,128)(2,1)}) %reduce-scatter.2.cloned.1.call-update) | async-done | bytes 786448 | tf_op jit(solution)/shard_map/reduce_scatter | solution.py:55
  402.8 2.3 copy.40
  405.1 4.6 %all-to-all-start.1 = ((bf16[32,12,1024]{2,1,0:T(8,128)(2,1)}), bf16[32,12,1024]{2,1,0:T(8,128)(2,1)S(1)}, u32[]{:S(2)}, u32[]{:S(2)}) async-start(bf16[32,12,1024]{2,1,0:T(8,128)(2,1)} %bitcast.17), calls=%async_computation.2 | async-start | bytes 2097152 | tf_op jit(solution)/shard_map/all_to_all | solution.py:58
  409.7 0.1 copy.33
  409.8 0.1 reshape.138
  409.9 0.1 copy.34
  410.0 25.7 %all-to-all-done.1 = bf16[32,12,1024]{2,1,0:T(8,128)(2,1)S(1)} async-done(((bf16[32,12,1024]{2,1,0:T(8,128)(2,1)}), bf16[32,12,1024]{2,1,0:T(8,128)(2,1)S(1)}, u32[]{:S(2)}, u32[]{:S(2)}) %all-to-all-start.1) | async-done | bytes 786464 | tf_op jit(solution)/shard_map/all_to_all | solution.py:58
  435.7 0.2 reshape.135
  435.9 0.2 pad_convert_fusion
  436.1 1.1 gather_fusion
  437.1 0.4 fusion.18
  437.5 1.6 add_bitcast_fusion
  (26 shorter events, 0.2 us)
Async XLA Ops:
  6.5 166.2 %copy-start = (bf16[1,32,1024]{2,1,0:T(8,128)(2,1)S(1)}, bf16[1,32,1024]{2,1,0:T(8,128)(2,1)}, u32[]{:S(2)}) copy-start(bf16[1,32,1024]{2,1,0:T(8,128)(2,1)} %param.10) | copy-start | bytes 196612
  6.5 154.7 %all-gather.6.cloned.1.call-start = ((), (), s32[]{:S(2)}) async-start(), calls=%async_computation.6 | async-start | bytes 10485760 | tf_op jit(solution)/shard_map/all_gather | solution.py:21
  7.3 216.1 %all-reduce.3.cloned.1.call-start = ((), (), s32[]{:S(2)}) async-start(), calls=%async_computation.3 | async-start | bytes 1048576 | tf_op jit(solution)/shard_map/psum | solution.py:26
  172.7 6.0 %copy-start.3 = (f32[1,32,1024]{2,1,0:T(8,128)S(1)}, f32[1,32,1024]{2,1,0:T(8,128)}, u32[]{:S(2)}) copy-start(f32[1,32,1024]{2,1,0:T(8,128)} %param.12) | copy-start | bytes 393220
  172.7 7.0 %copy-start.5 = (s32[1,32,8]{1,2,0:T(8,128)S(1)}, s32[1,32,8]{1,2,0:T(8,128)}, u32[]{:S(2)}) copy-start(s32[1,32,8]{1,2,0:T(8,128)} %param.15) | copy-start | bytes 3076
  172.7 7.0 %copy-start.6 = (s32[1,32,8]{1,2,0:T(8,128)S(1)}, s32[1,32,8]{1,2,0:T(8,128)}, u32[]{:S(2)}) copy-start(s32[1,32,8]{1,2,0:T(8,128)} %param.14) | copy-start | bytes 3076
  172.7 51.8 %dynamic-slice-start = ((f32[4096]{0:T(1024)}, s32[]{:T(128)}), f32[1024]{0:T(1024)S(1)}, s32[]{:S(2)}) async-start(f32[4096]{0:T(1024)} %param.13, s32[]{:T(128)} %select_n.51), calls=%async_computation.7 | async-start | bytes 8704 | tf_op jit(solution)/shard_map/dynamic_slice | solution.py:29
  178.8 0.8 copy-start.2
  179.6 129.9 %all-gather.4.cloned.1.call-start = ((), (), s32[]{:S(2)}) async-start(), calls=%async_computation.4 | async-start | bytes 5242880 | tf_op jit(solution)/shard_map/all_gather | solution.py:47
  259.3 143.5 %reduce-scatter.2.cloned.1.call-start = ((), (), s32[]{:S(2)}) async-start(), calls=%async_computation.5 | async-start | bytes 5242880 | tf_op jit(solution)/shard_map/reduce_scatter | solution.py:55
  350.0 59.9 %copy-start.4 = (f32[1,32,8]{1,2,0:T(8,128)S(1)}, f32[1,32,8]{1,2,0:T(8,128)}, u32[]{:S(2)}) copy-start(f32[1,32,8]{1,2,0:T(8,128)} %param.16) | copy-start | bytes 3076
  405.1 30.6 %all-to-all-start.1 = ((bf16[32,12,1024]{2,1,0:T(8,128)(2,1)}), bf16[32,12,1024]{2,1,0:T(8,128)(2,1)S(1)}, u32[]{:S(2)}, u32[]{:S(2)}) async-start(bf16[32,12,1024]{2,1,0:T(8,128)(2,1)} %bitcast.17), calls=%async_computation.2 | async-start | bytes 2097152 | tf_op jit(solution)/shard_map/all_to_all | solution.py:58
  435.9 3.2 copy-start.1
Sparse Core Ops, SparseCore 0:
  8.9 152.3 all-gather.5
  179.7 43.5 all-reduce.2
  259.5 50.0 all-gather.3
  350.2 52.5 reduce-scatter.1
